TPU v7x, 512 devices: a whole 4x4x16 slice. The times are simulated.
512 devices in a mesh: pair: 64 (over z, y), virt: 8 (over x, core).
Axes of the slice: x: 4, y: 4, z: 16, core: 2. Of those that a mesh axis runs over, the one named last changes fastest.
Arguments:
- amplitudes: bfloat16 [512, 8, 4096], P('pair', 'virt'), may hold values from -6 to 6
- partner: int32 [512], P('pair'), may hold values from 0 to 511, as said below
- integrals: bfloat16 [64, 4096, 4096], P('virt', 'pair'), may hold values from -0.09375 to 0.09375
- pattern: int32 [64], P('virt'), may hold values from 0 to 15, as said below
- owner: int32 [16], replicated, may hold values from 0 to 15, as said below
Outputs:
- ladder: bfloat16 [512, 16, 4096], P('pair', 'virt')
Inputs may be any that keep to these rules, and one draw needn't show every extreme that they name: partner pairs each pair with another one and is its own inverse; the partner of a pair held by index j of pair is held by index j + 64 / 2 modulo 64, that is half the pair axis away. `pattern`: every ab tile pair appears exactly four times in all. owner names every ab tile pair exactly once.
All inputs are finite; a program needn't handle non-finite values.
Results may differ from a plain program's by a relative error of at most 0.0051.
Values may be sent and summed in bfloat16 or wider, within the bound.
A program may use at most 64 MiB of HBM per device.

v0:
```python
import jax
import jax.numpy as jnp
from jax import lax
from jax.sharding import PartitionSpec as P

TILE = 64


def from_partner(value, axis, stride):
    mask = 2**stride
    pairs = [(source, source ^ mask) for source in range(lax.axis_size(axis))]
    return lax.ppermute(value, axis, pairs)


def symmetrize(plain, mirrored):
    count, width = (plain.shape[0], plain.shape[1])
    flipped = jnp.swapaxes(mirrored.reshape(count, width, TILE, TILE), 2, 3).reshape(plain.shape)
    return (plain.astype(jnp.float32) + flipped.astype(jnp.float32)).astype(jnp.bfloat16)


def shards(amplitudes, partner, integrals, pattern, owner):
    rows = amplitudes.shape[0]
    top_bit = lax.axis_size("pair").bit_length() - 2
    other = from_partner(amplitudes, "pair", top_bit)
    symmetric = symmetrize(amplitudes, jnp.take(other, partner % rows, axis=0))
    piece = lax.all_gather(symmetric, "pair", axis=0, tiled=True)
    flat = piece.reshape(piece.shape[0], -1)
    terms = jnp.einsum("rc,kjc->rkj", flat, integrals, preferred_element_type=jnp.float32)
    selector = (owner[None, :] == pattern[:, None]).astype(jnp.float32)
    spread = jnp.einsum("pkj,ks->psj", terms, selector, precision=lax.Precision.HIGHEST)
    routed = lax.all_to_all(spread, "pair", split_axis=0, concat_axis=2, tiled=True)
    summed = lax.psum_scatter(routed, "virt", scatter_dimension=1, tiled=True)
    result = summed.astype(jnp.bfloat16)
    return result


def solution(mesh):
    return jax.shard_map(
        shards,
        mesh=mesh,
        in_specs=(P("pair", "virt", None), P("pair"), P("virt", "pair", None), P("virt"), P()),
        out_specs=P("pair", "virt", None),
        check_vma=False,
    )
```

profile of v0, /device:TPU:1, one launch (start us, length us, event | category | flops | bytes accessed | tf_op | source)
XLA Modules:
  0.0 356.8 jit_solution(16470699635944835072)
XLA Ops:
  6.5 16.3 %collective-permute-start = (bf16[8,1,4096]{2,0,1:T(8,128)(2,1)}, bf16[8,1,4096]{2,0,1:T(8,128)(2,1)S(1)}, u32[]{:S(2)}, u32[]{:S(2)}) collective-permute-start(bf16[8,1,4096]{2,0,1:T(8,128)(2,1)} %param.5), channel_id=1, source_target_pairs={{0,256},{8,264},{16,272},{24,280},{32,288},{40,296},{48,304},{56,3... | collective-permute-start | bytes 196616 | tf_op jit(solution)/shard_map/ppermute | solution.py:12
  22.8 0.7 compare_and_fusion
  23.5 1.4 collective-permute-done
  24.9 0.6 gather_fusion
  25.4 0.2 gather.7
  25.6 0.1 copy.21
  25.8 0.1 convert_bitcast_fusion
  25.9 0.1 reshape.45
  26.0 1.5 add_convert_fusion
  27.5 0.0 reduce-scatter.2.cloned.1.call-start
  27.6 141.5 %all-gather.2.cloned.1.call-done = bf16[512,1,4096]{2,0,1:T(8,128)(2,1)} async-done(((bf16[8,1,4096]{2,0,1:T(8,128)(2,1)}), bf16[512,1,4096]{2,0,1:T(8,128)(2,1)}) %all-gather.2.cloned.1.call-update) | async-done | bytes 4194320 | tf_op jit(solution)/shard_map/all_gather | solution.py:26
  169.0 6.3 %fusion = f32[512,8,64]{0,1,2:T(8,128)S(1)} fusion(bf16[512,1,4096]{2,0,1:T(8,128)(2,1)} %all-gather.2.cloned.1.call-done, bf16[8,64,4096]{2,1,0:T(8,128)(2,1)} %param.7), kind=kOutput, calls=%fused_computation.1 | convolution fusion | flops 2147483648 | bytes 9437184 | tf_op jit(solution)/shard_map/rc,kjc->rkj/dot_general | solution.py:28
  175.4 1.1 convolution_bitcast_fusion
  176.5 4.2 %copy.23 = f32[512,16,64]{2,1,0:T(8,128)} copy(f32[512,16,64]{0,1,2:T(8,128)S(1)} %convolution_bitcast_fusion) | data formatting | bytes 4194304 | tf_op jit(solution)/shard_map/pkj,ks->psj/transpose | solution.py:30
  180.6 4.6 %reshape.61 = f32[64,1,8192]{2,1,0:T(1,128)S(1)} reshape(f32[512,16,64]{2,1,0:T(8,128)} %copy.23) | data formatting | bytes 4194304
  185.2 95.0 %all_to_all.18 = f32[64,1,8192]{2,1,0:T(1,128)} all-to-all(f32[64,1,8192]{2,1,0:T(1,128)S(1)} %reshape.61), channel_id=1, replica_groups=mesh['pair'=64,'virt'=8] {'pair'}, dimensions={0} | all-to-all | bytes 4194304 | tf_op jit(solution)/shard_map/all_to_all | solution.py:31
  280.2 0.5 broadcast.45
  280.7 7.5 %reduce = f32[64,8192]{1,0:T(8,128)S(1)} reduce(f32[64,1,8192]{2,1,0:T(1,128)} %all_to_all.18, f32[]{:T(128)} %broadcast.45), dimensions={1}, to_apply=%all_to_all.13.reduce_sub_computation | reduce | bytes 4194308 | tf_op jit(solution)/shard_map/all_to_all | solution.py:31
  288.2 3.0 reshape.62
  291.3 6.6 %copy.27 = f32[8,16,64,64]{3,2,0,1:T(8,128)} copy(f32[8,16,64,64]{3,1,0,2:T(8,128)} %bitcast.24) | data formatting | bytes 4194304 | tf_op jit(solution)/shard_map/all_to_all | solution.py:31
  297.8 4.8 %reshape.60 = f32[8,16,4096]{2,0,1:T(8,128)} reshape(f32[8,16,64,64]{3,2,0,1:T(8,128)} %copy.27) | data formatting | bytes 4194304 | tf_op jit(solution)/shard_map/all_to_all | solution.py:31
  302.6 45.6 %reduce-scatter.2.cloned.1.call-done = f32[8,2,4096]{2,0,1:T(8,128)} async-done(((f32[8,16,4096]{2,0,1:T(8,128)}), f32[8,2,4096]{2,0,1:T(8,128)}) %reduce-scatter.2.cloned.1.call-update) | async-done | bytes 262160 | tf_op jit(solution)/shard_map/reduce_scatter | solution.py:32
  348.2 1.0 convert_element_type.32
  349.2 0.8 copy.26
  (8 shorter events, 0.1 us)
Async XLA Ops:
  6.5 162.5 %all-gather.2.cloned.1.call-start = ((), (), s32[]{:S(2)}) async-start(), calls=%async_computation.2 | async-start | bytes 4259840 | tf_op jit(solution)/shard_map/all_gather | solution.py:26
  6.5 18.3 %collective-permute-start = (bf16[8,1,4096]{2,0,1:T(8,128)(2,1)}, bf16[8,1,4096]{2,0,1:T(8,128)(2,1)S(1)}, u32[]{:S(2)}, u32[]{:S(2)}) collective-permute-start(bf16[8,1,4096]{2,0,1:T(8,128)(2,1)} %param.5), channel_id=1, source_target_pairs={{0,256},{8,264},{16,272},{24,280},{32,288},{40,296},{48,304},{56,3... | collective-permute-start | bytes 196616 | tf_op jit(solution)/shard_map/ppermute | solution.py:12
  27.5 147.9 %copy-start = (s32[16]{0:T(128)S(1)}, s32[16]{0:T(128)}, u32[]{:S(2)}) copy-start(s32[16]{0:T(128)} %param.9) | copy-start | bytes 196
  27.5 147.9 %copy-start.1 = (s32[8]{0:T(128)S(1)}, s32[8]{0:T(128)}, u32[]{:S(2)}) copy-start(s32[8]{0:T(128)} %param.8) | copy-start | bytes 100
  27.5 320.7 %reduce-scatter.2.cloned.1.call-start = ((), (), s32[]{:S(2)}) async-start(), calls=%async_computation.3 | async-start | bytes 2359296 | tf_op jit(solution)/shard_map/reduce_scatter | solution.py:32
Sparse Core Ops, SparseCore 0:
  27.6 141.3 all-gather.1
  302.7 45.4 reduce-scatter.1
where the time goes:
time: 358 us; the launch traced here: 357 us
  waiting for transfers between devices  188 us (53%)
  blocking collectives  95 us (27%)
  local copies, waits for them, and re-layouts  25.4 us (7%)
  starting transfers between devices  16.3 us (5%)
  between operations  13.5 us (4%)
  other arithmetic  10.7 us (3%)
  matrix products  7.4 us (2%)
    all_gather x1, waiting for transfers between devices, shards(): piece = lax.all_gather(symmetric, 'pair', axis=0, tiled=True)  141 us
    all_to_all x1, blocking collectives, shards(): lax.all_to_all(spread, 'pair', split_axis=0, concat_axis=2, tiled=True)  95 us
    reduce_scatter x1, waiting for transfers between devices, shards(): summed = lax.psum_scatter(routed, 'virt', scatter_dimension=1, tiled=True)  45.6 us
    ppermute x1, starting transfers between devices, from_partner(): return lax.ppermute(value, axis, pairs)  16.3 us
    all_to_all x3, local copies, waits for them, and re-layouts, shards(): lax.all_to_all(spread, 'pair', split_axis=0, concat_axis=2, tiled=True)  11.8 us
    unnamed x6, local copies, waits for them, and re-layouts  7.61 us
    all_to_all x1, other arithmetic, shards(): lax.all_to_all(spread, 'pair', split_axis=0, concat_axis=2, tiled=True)  7.54 us
  transfers between devices with their start and end apart: 3, of which 3 were waited for; matrix products, arithmetic and copies ran while one was open for 0% of the time, Pallas kernels for 0%

commit v1 on v0

v1 whole, which is shorter than its diff:
```python
import jax
import jax.numpy as jnp
from jax import lax
from jax.experimental import pallas as pl
from jax.experimental.pallas import tpu as pltpu
from jax.sharding import PartitionSpec as P

MESH = pl.DeviceIdType.MESH
NZ, NY, NX = 16, 4, 4
ROWS = 8
TT = 4096
CUT = 1280
HALF = (TT - CUT) // 2
ORDER = (4, 12, 3, 13, 5, 11, 2, 14, 6, 10, 1, 15, 7, 9, 0, 8)
GROUPS = {4: (0, 2), 5: (2, 6), 6: (6, 10), 7: (10, 14), 8: (14, 16)}

ACOLS = pl.ds(0, CUT)
BCOLS = pl.ds(CUT, TT - CUT)
BHALF = {1: pl.ds(CUT, HALF), -1: pl.ds(CUT + HALF, HALF)}
AHALF = {1: pl.ds(0, CUT // 2), -1: pl.ds(CUT // 2, CUT // 2)}


def kernel(amp, ints, partner, pattern, owner, out, gath, tile, flip, acc, perm, masks,
           one_out, one_own, one_in, two_out, two_in, final, landed, load_sem, send, recv):
    pair = lax.axis_index("pair")
    virt = lax.axis_index("virt")
    z, y = pair // NY, pair % NY
    x, core = virt // 2, virt % 2

    def at(dz, dy):
        return ((z + (dz % NZ)) % NZ * NY + (y + (dy % NY)) % NY, virt)

    def beside(dx, swap):
        return (pair, (x + dx) % NX * 2 + (1 - core if swap else core))

    load = pltpu.make_async_copy(ints, tile, load_sem)
    load.start()

    counter = [0]
    table = {}

    def message(key, src, dst, device):
        if key not in table:
            slot = counter[0]
            counter[0] += 1
            table[key] = pltpu.make_async_remote_copy(
                src_ref=src, dst_ref=dst, send_sem=send.at[slot], recv_sem=recv.at[slot],
                device_id=device, device_id_type=MESH)
        return table[key]

    def z_b(s, way):
        cols = BHALF[way] if s == 8 else BCOLS
        return message(("zb", s, way), gath.at[(-way * (s - 1)) % NZ, 0, :, cols],
                       gath.at[(-way * s) % NZ, 0, :, cols], at(way, 0))

    def z_a(s, way, dy):
        return message(("za", s, way, dy), gath.at[(-way * (s - 1)) % NZ, dy, :, ACOLS],
                       gath.at[(-way * s) % NZ, dy, :, ACOLS], at(way, 0))

    def y_b(dz, way):
        dz %= NZ
        return message(("yb", dz, way), gath.at[dz, 0, :, BCOLS], gath.at[dz, -way % NY, :, BCOLS], at(0, way))

    def y_b2(dz, way):
        dz %= NZ
        return message(("yb2", dz, way), gath.at[dz, -way % NY, :, BHALF[way]], gath.at[dz, 2, :, BHALF[way]], at(0, way))

    def y_a(way):
        return message(("ya", way), gath.at[0, 0, :, ACOLS], gath.at[0, -way % NY, :, ACOLS], at(0, way))

    def y_a2(way):
        return message(("ya2", way), gath.at[0, -way % NY, :, AHALF[way]], gath.at[0, 2, :, AHALF[way]], at(0, way))

    def stage_one(step):
        lo, hi = GROUPS[step]
        return message(("one", step), one_out.at[:, lo:hi], one_in.at[:, lo:hi], beside(0, True))

    def stage_two(step, dx):
        lo, hi = GROUPS[step]
        return message(("two", step, dx), two_out.at[dx - 1, lo:hi], two_in.at[dx - 1, lo:hi], beside(dx, False))

    def deliver(position, dy):
        return message(("out", position, dy), final.at[position, dy], landed.at[pair], at(ORDER[position], dy))

    rows_iota = lax.broadcasted_iota(jnp.int32, (ROWS, 1), 0)
    lower = z < NZ // 2
    place = [jnp.where(lower, r, partner[r] % ROWS) for r in range(ROWS)]
    plain = amp[...].astype(jnp.float32)
    sorted_rows = jnp.zeros((ROWS, TT), jnp.float32)
    for r in range(ROWS):
        sorted_rows = jnp.where(rows_iota == place[r], plain[r:r + 1, :], sorted_rows)
    gath[0, 0] = sorted_rows.astype(jnp.bfloat16)

    barrier = pltpu.get_barrier_semaphore()
    friends = [at(1, 0), at(-1, 0), at(0, 1), at(0, -1), beside(0, True), beside(1, False), beside(2, False), beside(3, False)]
    for friend in friends:
        pl.semaphore_signal(barrier, inc=1, device_id=friend, device_id_type=MESH)

    lanes = lax.broadcasted_iota(jnp.int32, (1, 128), 1)
    for dx in range(NX):
        for c in range(2):
            to = (x + dx) % NX * 2 + (core if c == 0 else 1 - core)
            first, second = owner[2 * to], owner[2 * to + 1]
            for kk in range(4):
                even, odd = pattern[2 * kk], pattern[2 * kk + 1]

                def hit(tile_id, slot_id):
                    return jnp.where(tile_id == slot_id, jnp.float32(1), jnp.float32(0))

                masks[dx * 2 + c, pl.ds(2 * kk, 1), :] = jnp.where(lanes < 64, hit(even, first), hit(odd, second))
                masks[dx * 2 + c, pl.ds(2 * kk + 1, 1), :] = jnp.where(lanes < 64, hit(odd, first), hit(even, second))

    pl.semaphore_wait(barrier, len(friends))

    for way in (1, -1):
        z_b(1, way).start()
        y_a(way).start()
    for way in (1, -1):
        z_a(1, way, 0).start()
    for way in (1, -1):
        y_b(0, way).start()

    row = lax.broadcasted_iota(jnp.int32, (512, 512), 0)
    col = lax.broadcasted_iota(jnp.int32, (512, 512), 1)
    perm[...] = jnp.where(col == (row % 8) * 64 + row // 8, 1.0, 0.0).astype(jnp.bfloat16)
    load.wait()

    def flip_block(i):
        parts = []
        for h in range(2):
            cols = pl.ds(i * 1024 + h * 512, 512)
            turned = lax.dot_general(perm[...], tile[:, cols], (((1,), (1,)), ((), ())), preferred_element_type=jnp.float32)
            parts.append(turned.reshape(64, 8, 512))
        flip[:, pl.ds(i * 16, 16), :] = jnp.concatenate(parts, axis=1).astype(jnp.bfloat16)

    written = set()

    def compute(dzs, n):
        dzs = [dz % NZ for dz in dzs]
        left = jnp.concatenate([gath[dz].reshape(NY * ROWS, TT) for dz in dzs], axis=0)
        if n < 2:
            right = tile[pl.ds(n * 256, 256), :]
            got = lax.dot_general(left, right, (((1,), (1,)), ((), ())), preferred_element_type=jnp.float32)
        else:
            right = flip[:, :, pl.ds((n - 2) * 256, 256)].reshape(TT, 256)
            got = jnp.dot(left, right, preferred_element_type=jnp.float32)
        cols = pl.ds(n % 2 * 256, 256)
        for i, dz in enumerate(dzs):
            goal = dz if n < 2 else (dz + 8) % NZ
            value = got[i * 32:(i + 1) * 32]
            if (goal, n % 2) in written:
                acc[goal, :, cols] += value
            else:
                written.add((goal, n % 2))
                acc[goal, :, cols] = value

    def spread(step):
        lo, hi = GROUPS[step]
        for position in range(lo, hi):
            dz = ORDER[position]
            straight = [acc[dz, :, pl.ds(128 * kk, 128)] for kk in range(4)]
            turned = [pltpu.roll(v, 64, 1) for v in straight]
            for dx in range(NX):
                for c in range(2):
                    total = jnp.zeros((32, 128), jnp.float32)
                    for kk in range(4):
                        total += straight[kk] * masks[dx * 2 + c, pl.ds(2 * kk, 1), :]
                        total += turned[kk] * masks[dx * 2 + c, pl.ds(2 * kk + 1, 1), :]
                    if c == 0:
                        one_own[dx, position] = total
                    else:
                        one_out[dx, position] = total.astype(jnp.bfloat16)
        stage_one(step).start()

    def middle(step):
        lo, hi = GROUPS[step]
        stage_one(step).wait_recv()
        for dx in range(NX):
            for position in range(lo, hi):
                total = one_own[dx, position] + one_in[dx, position].astype(jnp.float32)
                if dx == 0:
                    one_own[0, position] = total
                else:
                    two_out[dx - 1, position] = total.astype(jnp.bfloat16)
            if dx:
                stage_two(step, dx).start()

    def finish(step):
        lo, hi = GROUPS[step]
        for dx in range(1, NX):
            stage_two(step, dx).wait_recv()
        for position in range(lo, hi):
            total = one_own[0, position]
            for dx in range(1, NX):
                total += two_in[dx - 1, position].astype(jnp.float32)
            final[position] = total.reshape(NY, ROWS, 128).astype(jnp.bfloat16)
            for dy in range(NY):
                if ORDER[position] or dy:
                    deliver(position, dy).start()
                else:
                    landed[pair] = total[:ROWS].astype(jnp.bfloat16)

    plan = {
        1: [lambda: flip_block(0), lambda: flip_block(1), lambda: flip_block(2), lambda: flip_block(3)],
        2: [lambda n=n: compute((0, 1, -1), n) for n in range(4)],
        3: [lambda n=n: compute((2, -2), n) for n in range(4)],
        4: [lambda n=n: compute((3, -3), n) for n in range(4)],
        5: [lambda n=n: compute((4, -4), n) for n in range(4)] + [lambda: spread(4)],
        6: [lambda n=n: compute((5, -5), n) for n in range(4)] + [lambda: spread(5), lambda: middle(4)],
        7: [lambda n=n: compute((6, -6), n) for n in range(4)] + [lambda: spread(6), lambda: (middle(5), finish(4))],
        8: [lambda n=n: compute((7, -7), n) for n in range(4)] + [lambda: spread(7), lambda: (middle(6), finish(5))],
    }

    def forward_first():
        for way in (1, -1):
            y_a(way).wait_recv()
            y_a2(way).start()
            for to in (1, -1):
                z_a(1, to, -way % NY).start()
        for way in (1, -1):
            y_b(0, way).wait_recv()
            y_b2(0, way).start()
        for way in (1, -1):
            y_a2(way).wait_recv()
        for to in (1, -1):
            z_a(1, to, 2).start()

    forward_first()
    for s in range(1, 8):
        jobs = plan[s]

        def job(i):
            if i < len(jobs):
                jobs[i]()

        for way in (1, -1):
            z_b(s, way).wait_recv()
            z_b(s + 1, way).start()
            for to in (1, -1):
                y_b(-way * s, to).start()
        for i, dy in enumerate((0, 1, 3, 2)):
            for way in (1, -1):
                z_a(s, way, dy).wait_recv()
                if s + 1 < 8 or (dy < 2) == (way == 1):
                    z_a(s + 1, way, dy).start()
            if i == 1:
                if s > 1:
                    for dz in (1 - s, s - 1):
                        for way in (1, -1):
                            y_b2(dz, way).wait_recv()
                else:
                    for way in (1, -1):
                        y_b2(0, way).wait_recv()
                job(0)
            if i == 2:
                job(1)
        for dz in (-s, s):
            for way in (1, -1):
                y_b(dz, way).wait_recv()
                y_b2(dz, way).start()
        for i in range(2, len(jobs)):
            job(i)

    for way in (1, -1):
        z_b(8, way).wait_recv()
    for way in (1, -1):
        y_b(8, way).start()
    for dz in (-7, 7):
        for way in (1, -1):
            y_b2(dz, way).wait_recv()
    plan[8][0]()
    plan[8][1]()
    for way in (1, -1):
        y_b(8, way).wait_recv()
        y_b2(8, way).start()
    for one in plan[8][2:]:
        one()
    for dy in range(NY):
        z_a(8, 1 if dy < 2 else -1, dy).wait_recv()
    for way in (1, -1):
        y_b2(8, way).wait_recv()
    for n in range(4):
        compute((8,), n)
    spread(8)
    middle(7)
    finish(6)
    middle(8)
    finish(7)
    finish(8)

    for position in range(NZ):
        for dy in range(NY):
            if ORDER[position] or dy:
                deliver(position, dy).wait_recv()

    natural = jnp.zeros((ROWS, 1), jnp.int32)
    for r in range(ROWS):
        natural = jnp.where(rows_iota == r, place[r], natural)
    low = lax.broadcasted_iota(jnp.int32, (ROWS, 128), 1) < 64
    for m in range(32):
        blocks = []
        for j in (2 * m, 2 * m + 1):
            found = landed[j].astype(jnp.float32)
            picked = jnp.zeros((ROWS, 128), jnp.float32)
            for i in range(ROWS):
                picked = jnp.where(natural == i, found[i:i + 1, :], picked)
            blocks.append(picked)
        cols = pl.ds(128 * m, 128)
        out[0, :, cols] = jnp.where(low, blocks[0], pltpu.roll(blocks[1], 64, 1)).astype(jnp.bfloat16)
        out[1, :, cols] = jnp.where(low, pltpu.roll(blocks[0], 64, 1), blocks[1]).astype(jnp.bfloat16)

    for one in table.values():
        one.wait_send()


MESSAGES = 16 + 60 + 32 + 32 + 4 + 5 + 15 + 63


def shards(amplitudes, partner, integrals, pattern, owner):
    vmem = pl.BlockSpec(memory_space=pltpu.VMEM)
    smem = pl.BlockSpec(memory_space=pltpu.SMEM)
    result = pl.pallas_call(
        kernel,
        out_shape=jax.ShapeDtypeStruct((2, ROWS, TT), jnp.bfloat16),
        in_specs=[vmem, pl.BlockSpec(memory_space=pl.ANY), smem, smem, smem],
        out_specs=vmem,
        scratch_shapes=[
            pltpu.VMEM((NZ, NY, ROWS, TT), jnp.bfloat16),
            pltpu.VMEM((512, TT), jnp.bfloat16),
            pltpu.VMEM((64, 64, 512), jnp.bfloat16),
            pltpu.VMEM((NZ, 32, 512), jnp.float32),
            pltpu.VMEM((512, 512), jnp.bfloat16),
            pltpu.VMEM((8, 8, 128), jnp.float32),
            pltpu.VMEM((NX, NZ, 32, 128), jnp.bfloat16),
            pltpu.VMEM((NX, NZ, 32, 128), jnp.float32),
            pltpu.VMEM((NX, NZ, 32, 128), jnp.bfloat16),
            pltpu.VMEM((NX - 1, NZ, 32, 128), jnp.bfloat16),
            pltpu.VMEM((NX - 1, NZ, 32, 128), jnp.bfloat16),
            pltpu.VMEM((NZ, NY, ROWS, 128), jnp.bfloat16),
            pltpu.VMEM((NZ * NY, ROWS, 128), jnp.bfloat16),
            pltpu.SemaphoreType.DMA,
            pltpu.SemaphoreType.DMA((MESSAGES,)),
            pltpu.SemaphoreType.DMA((MESSAGES,)),
        ],
        compiler_params=pltpu.CompilerParams(collective_id=0, has_side_effects=True, vmem_limit_bytes=60 * 2**20),
    )(amplitudes.reshape(ROWS, TT), integrals.reshape(512, TT), partner, pattern, owner)
    return jnp.swapaxes(result, 0, 1)


def solution(mesh):
    return jax.shard_map(
        shards,
        mesh=mesh,
        in_specs=(P("pair", "virt", None), P("pair"), P("virt", "pair", None), P("virt"), P()),
        out_specs=P("pair", "virt", None),
        check_vma=False,
    )
```

time: 358 us -> 92 us (0.26)
  waiting for transfers between devices: 188 us -> 0 us
  blocking collectives: 95 us -> 0 us
  Pallas kernels: 0 us -> 90.1 us
  local copies, waits for them, and re-layouts: 25.4 us -> 1.7 us
  starting transfers between devices: 16.3 us -> 0 us
  between operations: 13.5 us -> 0.01 us
  other arithmetic: 10.7 us -> 0 us
  matrix products: 7.4 us -> 0 us
    all_gather x1 -> x0, waiting for transfers between devices: 141 us -> none  [shards(): piece = lax.all_gather(symmetric, 'pair', axis=0, tiled=True)]
    all_to_all x1 -> x0, blocking collectives: 95 us -> none  [shards(): lax.all_to_all(spread, 'pair', split_axis=0, concat_axis=2, tiled=True)]
    pallas_call x0 -> x1, Pallas kernels: none -> 90.1 us  [shards(): pl.pallas_call(kernel, out_shape=jax.ShapeDtypeStruct((2, ROWS, TT), jnp....]
    reduce_scatter x1 -> x0, waiting for transfers between devices: 45.6 us -> none  [shards(): summed = lax.psum_scatter(routed, 'virt', scatter_dimension=1, tiled=True)]
    ppermute x1 -> x0, starting transfers between devices: 16.3 us -> none  [from_partner(): return lax.ppermute(value, axis, pairs)]
    all_to_all x3 -> x0, local copies, waits for them, and re-layouts: 11.8 us -> none  [shards(): lax.all_to_all(spread, 'pair', split_axis=0, concat_axis=2, tiled=True)]
    unnamed x6 -> x0, local copies, waits for them, and re-layouts: 7.61 us -> none
    all_to_all x1 -> x0, other arithmetic: 7.54 us -> none  [shards(): lax.all_to_all(spread, 'pair', split_axis=0, concat_axis=2, tiled=True)]
  transfers between devices with their start and end apart: 3 -> 0, of which waited for: 3 -> 0; matrix products, arithmetic and copies ran while one was open for 0% -> 0% of each run, Pallas kernels for 0% -> 0%
where the time goes in v1:
time: 92 us; the launch traced here: 91.8 us
  Pallas kernels  90.1 us (98%)
  local copies, waits for them, and re-layouts  1.7 us (2%)
    pallas_call x1, Pallas kernels, shards(): pl.pallas_call(kernel, out_shape=jax.ShapeDtypeStruct((2, ROWS, TT), jnp....  90.1 us

profile of v1, /device:TPU:1, one launch (start us, length us, event | category | flops | bytes accessed | tf_op | source)
XLA Modules:
  0.0 91.8 jit_solution(2706870349117543976)
XLA Ops:
  0.0 90.1 %shard_map.55 = bf16[2,8,4096]{2,1,0:T(8,128)(2,1)} custom-call(bf16[8,4096]{1,0:T(8,128)(2,1)} %bitcast.5, bf16[512,4096]{1,0:T(8,128)(2,1)} %bitcast.3, s32[8]{0:T(128)} %partner.1, s32[8]{0:T(128)} %pattern.1, s32[16]{0:T(128)} %owner.1), custom_call_target="tpu_custom_call" | custom-call | tf_op jit(solution)/shard_map/pallas_call | solution.py:322
  90.1 1.7 %copy.6 = bf16[8,2,4096]{2,1,0:T(2,128)(2,1)} copy(bf16[8,2,4096]{2,0,1:T(8,128)(2,1)} %bitcast.4) | data formatting | bytes 262144 | tf_op jit(solution)/shard_map/transpose | solution.py:347

commit v2 on v1

v2 whole, which is shorter than its diff:
```python
import jax
import jax.numpy as jnp
from jax import lax
from jax.experimental import pallas as pl
from jax.experimental.pallas import tpu as pltpu
from jax.sharding import PartitionSpec as P

MESH = pl.DeviceIdType.MESH
NZ, NY, NX = 16, 4, 4
NB = NZ // 2
ROWS = 8
TT = 4096
CUT = 1536
HALF = (TT - CUT) // 2
ORDER = (0, 1, 7, 2, 6, 3, 5, 4)
GROUPS = ((0, 1), (1, 3), (3, 5), (5, 7), (7, 8))

ACOLS = pl.ds(0, CUT)
BCOLS = pl.ds(CUT, TT - CUT)
BHALF = {1: pl.ds(CUT, HALF), -1: pl.ds(CUT + HALF, HALF)}


def kernel(amp, ints, partner, pattern, owner, out, mine, met, gath, tile, flip, acc, perm, masks,
           one_out, one_own, one_in, two_out, two_in, final, landed, load_sem, send, recv):
    pair = lax.axis_index("pair")
    virt = lax.axis_index("virt")
    z, y = pair // NY, pair % NY
    x, core = virt // 2, virt % 2

    def at(dz, dy):
        return ((z + (dz % NZ)) % NZ * NY + (y + (dy % NY)) % NY, virt)

    def beside(dx, swap):
        return (pair, (x + dx) % NX * 2 + (1 - core if swap else core))

    load = pltpu.make_async_copy(ints, tile, load_sem)
    load.start()

    table = {}

    def message(key, src, dst, device):
        if key not in table:
            slot = len(table)
            table[key] = pltpu.make_async_remote_copy(
                src_ref=src, dst_ref=dst, send_sem=send.at[slot], recv_sem=recv.at[slot],
                device_id=device, device_id_type=MESH)
        return table[key]

    def meet(part, way):
        cols = ACOLS if part == 0 else BCOLS
        return message(("meet", part, way), mine.at[:, cols], met.at[(1 - way) // 2, :, cols], at(4 * way, 0))

    def z_b(far, way):
        if far < 3:
            return message(("zb", far, way), gath.at[0, 0, :, BCOLS], gath.at[(-way * far) % NB, 0, :, BCOLS], at(way * far, 0))
        cols = BCOLS if far == 3 else BHALF[way]
        return message(("zb", far, way), gath.at[(-way * 2) % NB, 0, :, cols],
                       gath.at[(-way * far) % NB, 0, :, cols], at(way * (far - 2), 0))

    def z_a(s, way, dy):
        return message(("za", s, way, dy), gath.at[(-way * (s - 1)) % NB, dy, :, ACOLS],
                       gath.at[(-way * s) % NB, dy, :, ACOLS], at(way, 0))

    def y_b(dz, way):
        dz %= NB
        return message(("yb", dz, way), gath.at[dz, 0, :, BCOLS], gath.at[dz, -way % NY, :, BCOLS], at(0, way))

    def y_b2(dz, way):
        dz %= NB
        return message(("yb2", dz, way), gath.at[dz, -way % NY, :, BHALF[way]], gath.at[dz, 2, :, BHALF[way]], at(0, way))

    def y_a(way):
        return message(("ya", way), gath.at[0, 0, :, ACOLS], gath.at[0, -way % NY, :, ACOLS], at(0, way))

    def stage_one(group):
        lo, hi = GROUPS[group]
        return message(("one", group), one_out.at[:, 2 * lo:2 * hi], one_in.at[:, 2 * lo:2 * hi], beside(0, True))

    def stage_two(group, dx):
        lo, hi = GROUPS[group]
        return message(("two", group, dx), two_out.at[dx - 1, 2 * lo:2 * hi], two_in.at[dx - 1, 2 * lo:2 * hi], beside(dx, False))

    def upper(dz):
        return (z + (dz % NZ)) % NZ // NB

    def deliver(index, side, dy):
        dz = ORDER[index] + 4 * side
        return message(("out", index, side, dy), final.at[2 * index + upper(dz), dy], landed.at[pair], at(dz, dy))

    rows_iota = lax.broadcasted_iota(jnp.int32, (ROWS, 1), 0)
    lower = z < NB
    place = [jnp.where(lower, r, partner[r] % ROWS) for r in range(ROWS)]
    plain = amp[...].astype(jnp.float32)
    sorted_rows = jnp.zeros((ROWS, TT), jnp.float32)
    for r in range(ROWS):
        sorted_rows = jnp.where(rows_iota == place[r], plain[r:r + 1, :], sorted_rows)
    mine[...] = sorted_rows.astype(jnp.bfloat16)

    barrier = pltpu.get_barrier_semaphore()
    friends = [at(4, 0), at(-4, 0), at(1, 0), at(-1, 0), at(2, 0), at(-2, 0), at(0, 1), at(0, -1), at(0, 2),
               beside(0, True), beside(1, False), beside(2, False), beside(3, False)]
    for friend in friends:
        pl.semaphore_signal(barrier, inc=1, device_id=friend, device_id_type=MESH)

    lanes = lax.broadcasted_iota(jnp.int32, (1, 128), 1)
    for dx in range(NX):
        for c in range(2):
            to = (x + dx) % NX * 2 + (core if c == 0 else 1 - core)
            first, second = owner[2 * to], owner[2 * to + 1]
            for kk in range(4):
                even, odd = pattern[2 * kk], pattern[2 * kk + 1]

                def hit(tile_id, slot_id):
                    return jnp.where(tile_id == slot_id, jnp.float32(1), jnp.float32(0))

                masks[dx * 2 + c, pl.ds(2 * kk, 1), :] = jnp.where(lanes < 64, hit(even, first), hit(odd, second))
                masks[dx * 2 + c, pl.ds(2 * kk + 1, 1), :] = jnp.where(lanes < 64, hit(odd, first), hit(even, second))

    pl.semaphore_wait(barrier, len(friends))
    for part in range(2):
        for way in (1, -1):
            meet(part, way).start()

    row = lax.broadcasted_iota(jnp.int32, (512, 512), 0)
    col = lax.broadcasted_iota(jnp.int32, (512, 512), 1)
    perm[...] = jnp.where(col == (row % 8) * 64 + row // 8, 1.0, 0.0).astype(jnp.bfloat16)
    load.wait()

    def flip_block(i):
        parts = []
        for h in range(2):
            cols = pl.ds(i * 1024 + h * 512, 512)
            turned = lax.dot_general(perm[...], tile[:, cols], (((1,), (1,)), ((), ())), preferred_element_type=jnp.float32)
            parts.append(turned.reshape(64, 8, 512))
        flip[:, pl.ds(i * 16, 16), :] = jnp.concatenate(parts, axis=1).astype(jnp.bfloat16)

    def compute(group, n):
        lo, hi = GROUPS[group]
        blocks = ORDER[lo:hi]
        left = jnp.concatenate([gath[dz].reshape(NY * ROWS, TT) for dz in blocks], axis=0)
        if n < 2:
            right = tile[pl.ds(n * 256, 256), :]
            got = lax.dot_general(left, right, (((1,), (1,)), ((), ())), preferred_element_type=jnp.float32)
        else:
            right = flip[:, :, pl.ds((n - 2) * 256, 256)].reshape(TT, 256)
            got = jnp.dot(left, right, preferred_element_type=jnp.float32)
        for i in range(len(blocks)):
            acc[2 * (lo + i) + n // 2, :, pl.ds(n % 2 * 256, 256)] = got[i * 32:(i + 1) * 32]

    def spread(group):
        lo, hi = GROUPS[group]
        for position in range(2 * lo, 2 * hi):
            straight = [acc[position, :, pl.ds(128 * kk, 128)] for kk in range(4)]
            turned = [pltpu.roll(v, 64, 1) for v in straight]
            for dx in range(NX):
                for c in range(2):
                    total = jnp.zeros((32, 128), jnp.float32)
                    for kk in range(4):
                        total += straight[kk] * masks[dx * 2 + c, pl.ds(2 * kk, 1), :]
                        total += turned[kk] * masks[dx * 2 + c, pl.ds(2 * kk + 1, 1), :]
                    if c == 0:
                        one_own[dx, position] = total
                    else:
                        one_out[dx, position] = total.astype(jnp.bfloat16)
        stage_one(group).start()

    def middle(group):
        lo, hi = GROUPS[group]
        stage_one(group).wait_recv()
        for dx in (1, 2, 3, 0):
            for position in range(2 * lo, 2 * hi):
                total = one_own[dx, position] + one_in[dx, position].astype(jnp.float32)
                if dx == 0:
                    one_own[0, position] = total
                else:
                    two_out[dx - 1, position] = total.astype(jnp.bfloat16)
            if dx:
                stage_two(group, dx).start()

    def finish(group):
        lo, hi = GROUPS[group]
        for dx in range(1, NX):
            stage_two(group, dx).wait_recv()
        for position in range(2 * lo, 2 * hi):
            total = one_own[0, position]
            for dx in range(1, NX):
                total += two_in[dx - 1, position].astype(jnp.float32)
            final[position] = total.reshape(NY, ROWS, 128).astype(jnp.bfloat16)
        for index in range(lo, hi):
            for side in (1, -1):
                for dy in (2, 1, 3, 0):
                    if (ORDER[index] + 4 * side) % NZ or dy:
                        deliver(index, side, dy).start()
                    else:
                        landed[pair] = final[2 * index + upper(0), 0]

    def add_up(cols):
        gath[0, 0, :, cols] = (met[0, :, cols].astype(jnp.float32) + met[1, :, cols].astype(jnp.float32)).astype(jnp.bfloat16)

    def pass_b(*blocks):
        for dz in blocks:
            for way in (1, -1):
                y_b(dz, way).start()

    def relay_b(*blocks):
        for dz in blocks:
            for way in (1, -1):
                y_b(dz, way).wait_recv()
                y_b2(dz, way).start()

    def whole_b(*blocks):
        for dz in blocks:
            for way in (1, -1):
                y_b2(dz, way).wait_recv()

    def ways(s, dy):
        return (1, -1) if s < 4 else ((1,) if dy < 2 else (-1,))

    def relay_a(s):
        for dy in (0, 1, 3, 2):
            for way in ways(s, dy):
                z_a(s, way, dy).wait_recv()
                if s < 4 and way in ways(s + 1, dy):
                    z_a(s + 1, way, dy).start()

    for i in range(3):
        flip_block(i)

    for way in (1, -1):
        meet(0, way).wait_recv()
    add_up(ACOLS)
    for way in (1, -1, 2):
        y_a(way).start()
    for way in (1, -1):
        meet(1, way).wait_recv()
    add_up(BCOLS)
    for way in (1, -1):
        z_b(2, way).start()
        z_b(1, way).start()
    for way in (1, -1):
        z_a(1, way, 0).start()
    pass_b(0)
    for way in (1, -1, 2):
        y_a(way).wait_recv()
        for to in (1, -1):
            z_a(1, to, -way % NY).start()

    flip_block(3)
    for way in (1, -1):
        z_b(1, way).wait_recv()
    pass_b(1, -1)
    for way in (1, -1):
        z_b(2, way).wait_recv()
        z_b(4, way).start()
        z_b(3, way).start()
    relay_b(0)
    pass_b(2, -2)
    relay_a(1)
    whole_b(0)
    compute(0, 0)
    compute(0, 1)
    relay_b(1, -1)
    compute(0, 2)
    compute(0, 3)
    for way in (1, -1):
        z_b(4, way).wait_recv()
        z_b(3, way).wait_recv()
    pass_b(4, 3, -3)
    relay_a(2)
    relay_b(2, -2)
    spread(0)
    whole_b(1, -1)
    compute(1, 0)
    compute(1, 1)
    relay_b(4, 3, -3)
    relay_a(3)
    compute(1, 2)
    compute(1, 3)
    spread(1)
    middle(0)
    whole_b(2, -2)
    for n in range(4):
        compute(2, n)
    spread(2)
    middle(1)
    finish(0)
    whole_b(3, -3)
    for n in range(4):
        compute(3, n)
    spread(3)
    middle(2)
    finish(1)
    relay_a(4)
    whole_b(4)
    for n in range(4):
        compute(4, n)
    spread(4)
    middle(3)
    finish(2)
    middle(4)
    finish(3)
    finish(4)

    for index in range(NB):
        for side in (1, -1):
            for dy in range(NY):
                if (ORDER[index] + 4 * side) % NZ or dy:
                    deliver(index, side, dy).wait_recv()

    natural = jnp.zeros((ROWS, 1), jnp.int32)
    for r in range(ROWS):
        natural = jnp.where(rows_iota == r, place[r], natural)
    low = lax.broadcasted_iota(jnp.int32, (ROWS, 128), 1) < 64
    for m in range(32):
        blocks = []
        for j in (2 * m, 2 * m + 1):
            found = landed[j].astype(jnp.float32)
            picked = jnp.zeros((ROWS, 128), jnp.float32)
            for i in range(ROWS):
                picked = jnp.where(natural == i, found[i:i + 1, :], picked)
            blocks.append(picked)
        cols = pl.ds(128 * m, 128)
        out[0, :, cols] = jnp.where(low, blocks[0], pltpu.roll(blocks[1], 64, 1)).astype(jnp.bfloat16)
        out[1, :, cols] = jnp.where(low, pltpu.roll(blocks[0], 64, 1), blocks[1]).astype(jnp.bfloat16)

    for one in table.values():
        one.wait_send()


MESSAGES = 4 + 8 + 28 + 16 + 16 + 3 + 5 + 15 + 63


def shards(amplitudes, partner, integrals, pattern, owner):
    plain = amplitudes.reshape(ROWS, TT)
    turned = jnp.swapaxes(plain.reshape(ROWS, 64, 64), 1, 2).reshape(ROWS, TT)
    plain = jnp.where(lax.axis_index("pair") < NB * NY, plain, turned)
    vmem = pl.BlockSpec(memory_space=pltpu.VMEM)
    smem = pl.BlockSpec(memory_space=pltpu.SMEM)
    result = pl.pallas_call(
        kernel,
        out_shape=jax.ShapeDtypeStruct((2, ROWS, TT), jnp.bfloat16),
        in_specs=[vmem, pl.BlockSpec(memory_space=pl.ANY), smem, smem, smem],
        out_specs=vmem,
        scratch_shapes=[
            pltpu.VMEM((ROWS, TT), jnp.bfloat16),
            pltpu.VMEM((2, ROWS, TT), jnp.bfloat16),
            pltpu.VMEM((NB, NY, ROWS, TT), jnp.bfloat16),
            pltpu.VMEM((512, TT), jnp.bfloat16),
            pltpu.VMEM((64, 64, 512), jnp.bfloat16),
            pltpu.VMEM((NZ, 32, 512), jnp.float32),
            pltpu.VMEM((512, 512), jnp.bfloat16),
            pltpu.VMEM((8, 8, 128), jnp.float32),
            pltpu.VMEM((NX, NZ, 32, 128), jnp.bfloat16),
            pltpu.VMEM((NX, NZ, 32, 128), jnp.float32),
            pltpu.VMEM((NX, NZ, 32, 128), jnp.bfloat16),
            pltpu.VMEM((NX - 1, NZ, 32, 128), jnp.bfloat16),
            pltpu.VMEM((NX - 1, NZ, 32, 128), jnp.bfloat16),
            pltpu.VMEM((NZ, NY, ROWS, 128), jnp.bfloat16),
            pltpu.VMEM((NZ * NY, ROWS, 128), jnp.bfloat16),
            pltpu.SemaphoreType.DMA,
            pltpu.SemaphoreType.DMA((MESSAGES,)),
            pltpu.SemaphoreType.DMA((MESSAGES,)),
        ],
        compiler_params=pltpu.CompilerParams(collective_id=0, has_side_effects=True, vmem_limit_bytes=60 * 2**20),
    )(plain, integrals.reshape(512, TT), partner, pattern, owner)
    return jnp.swapaxes(result, 0, 1)


def solution(mesh):
    return jax.shard_map(
        shards,
        mesh=mesh,
        in_specs=(P("pair", "virt", None), P("pair"), P("virt", "pair", None), P("virt"), P()),
        out_specs=P("pair", "virt", None),
        check_vma=False,
    )
```

time: 92 us -> 72.2 us (0.78)
  Pallas kernels: 90.1 us -> 67.1 us
  other arithmetic: 0 us -> 1.48 us
  local copies, waits for them, and re-layouts: 1.7 us -> 3.03 us
    pallas_call x1, Pallas kernels: 90.1 us -> 67.1 us  [shards(): pl.pallas_call(kernel, out_shape=jax.ShapeDtypeStruct((2, ROWS, TT), jnp....]
    select_n x0 -> x1, other arithmetic: none -> 1.48 us  [shards(): plain = jnp.where(lax.axis_index('pair') < NB * NY, plain, turned)]
    another operation x0 -> x2, local copies, waits for them, and re-layouts: none -> 1.15 us  [shards(): turned = jnp.swapaxes(plain.reshape(ROWS, 64, 64), 1, 2).reshape(ROWS, TT)]
where the time goes in v2:
time: 72.2 us; the launch traced here: 71.7 us
  Pallas kernels  67.1 us (93%)
  local copies, waits for them, and re-layouts  3.03 us (4%)
  other arithmetic  1.48 us (2%)
    pallas_call x1, Pallas kernels, shards(): pl.pallas_call(kernel, out_shape=jax.ShapeDtypeStruct((2, ROWS, TT), jnp....  67.1 us
    transpose x1, local copies, waits for them, and re-layouts, shards(): return jnp.swapaxes(result, 0, 1)  1.7 us
    select_n x1, other arithmetic, shards(): plain = jnp.where(lax.axis_index('pair') < NB * NY, plain, turned)  1.48 us

profile of v2, /device:TPU:1, one launch (start us, length us, event | category | flops | bytes accessed | tf_op | source)
XLA Modules:
  0.0 71.7 jit_solution(3102386449856517293)
XLA Ops:
  0.0 1.0 %reshape_reshape.3 = bf16[8,64,64]{2,1,0:T(8,128)(2,1)S(1)} reshape(bf16[8,1,4096]{2,0,1:T(8,128)(2,1)} %param.5) | data formatting | bytes 131072 | tf_op jit(solution)/shard_map/reshape;reshape | solution.py:335
  1.0 0.1 copy.6
  1.2 0.2 reshape.10
  1.4 1.5 %bitcast_select_fusion.amp = bf16[8,4096]{1,0:T(8,128)(2,1)} fusion(bf16[8,4096]{1,0:T(8,128)(2,1)S(1)} %reshape.10, bf16[8,1,4096]{2,0,1:T(8,128)(2,1)} %param.5, pred[]{:T(512)S(6)} %lt.3), kind=kLoop, calls=%fused_computation | loop fusion | flops 32768 | bytes 196609 | tf_op jit(solution)/shard_map/jit(_where)/select_n | solution.py:336
  2.8 67.1 %shard_map.55 = bf16[2,8,4096]{2,1,0:T(8,128)(2,1)} custom-call(bf16[8,4096]{1,0:T(8,128)(2,1)} %bitcast_select_fusion.amp, bf16[512,4096]{1,0:T(8,128)(2,1)} %bitcast.7, s32[8]{0:T(128)} %partner.1, s32[8]{0:T(128)} %pattern.1, s32[16]{0:T(128)} %owner.1), custom_call_target="tpu_custom_call" | custom-call | tf_op jit(solution)/shard_map/pallas_call | solution.py:339
  70.0 1.7 %copy.7 = bf16[8,2,4096]{2,1,0:T(2,128)(2,1)} copy(bf16[8,2,4096]{2,0,1:T(8,128)(2,1)} %bitcast.8) | data formatting | bytes 262144 | tf_op jit(solution)/shard_map/transpose | solution.py:366

commit v3 on v2

--- a/solution.py
+++ b/solution.py
@@ -13,7 +13,7 @@
 CUT = 1536
 HALF = (TT - CUT) // 2
 ORDER = (0, 1, 7, 2, 6, 3, 5, 4)
-GROUPS = ((0, 1), (1, 3), (3, 5), (5, 7), (7, 8))
+GROUPS = ((0, 1), (1, 3), (3, 5), (5, 8))
 
 ACOLS = pl.ds(0, CUT)
 BCOLS = pl.ds(CUT, TT - CUT)
@@ -57,9 +57,10 @@
         return message(("zb", far, way), gath.at[(-way * 2) % NB, 0, :, cols],
                        gath.at[(-way * far) % NB, 0, :, cols], at(way * (far - 2), 0))
 
-    def z_a(s, way, dy):
-        return message(("za", s, way, dy), gath.at[(-way * (s - 1)) % NB, dy, :, ACOLS],
-                       gath.at[(-way * s) % NB, dy, :, ACOLS], at(way, 0))
+    def z_a(far, way, dy):
+        origin = 0 if far < 3 else (-way * 2) % NB
+        return message(("za", far, way, dy), gath.at[origin, dy, :, ACOLS],
+                       gath.at[(-way * far) % NB, dy, :, ACOLS], at(way * (far if far < 3 else far - 2), 0))
 
     def y_b(dz, way):
         dz %= NB
@@ -87,6 +88,15 @@
         dz = ORDER[index] + 4 * side
         return message(("out", index, side, dy), final.at[2 * index + upper(dz), dy], landed.at[pair], at(dz, dy))
 
+    barrier = pltpu.get_barrier_semaphore()
+    friends = [at(4, 0), at(-4, 0), at(1, 0), at(-1, 0), at(2, 0), at(-2, 0), at(0, 1), at(0, -1), at(0, 2),
+               beside(0, True), beside(1, False), beside(2, False), beside(3, False)]
+    for friend in friends:
+        pl.semaphore_signal(barrier, inc=1, device_id=friend, device_id_type=MESH)
+
+    row = lax.broadcasted_iota(jnp.int32, (512, 512), 0)
+    col = lax.broadcasted_iota(jnp.int32, (512, 512), 1)
+    perm[...] = jnp.where(col == (row % 8) * 64 + row // 8, 1.0, 0.0).astype(jnp.bfloat16)
     rows_iota = lax.broadcasted_iota(jnp.int32, (ROWS, 1), 0)
     lower = z < NB
     place = [jnp.where(lower, r, partner[r] % ROWS) for r in range(ROWS)]
@@ -94,13 +104,30 @@
     sorted_rows = jnp.zeros((ROWS, TT), jnp.float32)
     for r in range(ROWS):
         sorted_rows = jnp.where(rows_iota == place[r], plain[r:r + 1, :], sorted_rows)
-    mine[...] = sorted_rows.astype(jnp.bfloat16)
-
-    barrier = pltpu.get_barrier_semaphore()
-    friends = [at(4, 0), at(-4, 0), at(1, 0), at(-1, 0), at(2, 0), at(-2, 0), at(0, 1), at(0, -1), at(0, 2),
-               beside(0, True), beside(1, False), beside(2, False), beside(3, False)]
-    for friend in friends:
-        pl.semaphore_signal(barrier, inc=1, device_id=friend, device_id_type=MESH)
+
+    def exchange(value, order):
+        return lax.dot_general(value.astype(jnp.bfloat16), order, (((1,), (1,)), ((), ())), preferred_element_type=jnp.float32)
+
+    low = lax.broadcasted_iota(jnp.int32, (ROWS, 128), 1) < 64
+    stacked = jnp.concatenate([sorted_rows[:, 512 * b:512 * (b + 1)] for b in range(8)], axis=0)
+    once = exchange(stacked, perm[...])
+    regrouped = []
+    for e in range(8):
+        pieces = []
+        for k in range(4):
+            first = once[16 * k:16 * k + 8, 128 * (e // 2):128 * (e // 2 + 1)]
+            second = once[16 * k + 8:16 * k + 16, 128 * (e // 2):128 * (e // 2 + 1)]
+            if e % 2:
+                pieces.append(jnp.where(low, pltpu.roll(first, 64, 1), second))
+            else:
+                pieces.append(jnp.where(low, first, pltpu.roll(second, 64, 1)))
+        regrouped.append(jnp.concatenate(pieces, axis=1))
+    second_order = jnp.where(col == row % 64 // 8 * 64 + row // 64 * 8 + row % 8, 1.0, 0.0).astype(jnp.bfloat16)
+    twice = exchange(jnp.concatenate(regrouped, axis=0), second_order)
+    for e in range(8):
+        cols = pl.ds(512 * e, 512)
+        mine[:, cols] = jnp.where(lower, sorted_rows[:, 512 * e:512 * (e + 1)], twice[8 * e:8 * (e + 1)]).astype(jnp.bfloat16)
+
 
     lanes = lax.broadcasted_iota(jnp.int32, (1, 128), 1)
     for dx in range(NX):
@@ -121,9 +148,6 @@
         for way in (1, -1):
             meet(part, way).start()
 
-    row = lax.broadcasted_iota(jnp.int32, (512, 512), 0)
-    col = lax.broadcasted_iota(jnp.int32, (512, 512), 1)
-    perm[...] = jnp.where(col == (row % 8) * 64 + row // 8, 1.0, 0.0).astype(jnp.bfloat16)
     load.wait()
 
     def flip_block(i):
@@ -213,15 +237,26 @@
             for way in (1, -1):
                 y_b2(dz, way).wait_recv()
 
-    def ways(s, dy):
-        return (1, -1) if s < 4 else ((1,) if dy < 2 else (-1,))
-
-    def relay_a(s):
-        for dy in (0, 1, 3, 2):
-            for way in ways(s, dy):
-                z_a(s, way, dy).wait_recv()
-                if s < 4 and way in ways(s + 1, dy):
-                    z_a(s + 1, way, dy).start()
+    def ends_a(dy):
+        return 1 if dy < 2 else -1
+
+    def send_a(dy):
+        for far in (2, 1):
+            for way in (1, -1):
+                z_a(far, way, dy).start()
+
+    def relay_a(*dys):
+        for dy in dys:
+            for way in (1, -1):
+                z_a(2, way, dy).wait_recv()
+                if way == ends_a(dy):
+                    z_a(4, way, dy).start()
+                z_a(3, way, dy).start()
+
+    def whole_a(far):
+        for dy in range(NY):
+            for way in (1, -1) if far < 4 else (ends_a(dy),):
+                z_a(far, way, dy).wait_recv()
 
     for i in range(3):
         flip_block(i)
@@ -231,49 +266,47 @@
     add_up(ACOLS)
     for way in (1, -1, 2):
         y_a(way).start()
+    send_a(0)
     for way in (1, -1):
         meet(1, way).wait_recv()
     add_up(BCOLS)
     for way in (1, -1):
         z_b(2, way).start()
         z_b(1, way).start()
-    for way in (1, -1):
-        z_a(1, way, 0).start()
     pass_b(0)
     for way in (1, -1, 2):
         y_a(way).wait_recv()
-        for to in (1, -1):
-            z_a(1, to, -way % NY).start()
+        send_a(-way % NY)
 
     flip_block(3)
     for way in (1, -1):
         z_b(1, way).wait_recv()
     pass_b(1, -1)
+    relay_a(0)
     for way in (1, -1):
         z_b(2, way).wait_recv()
         z_b(4, way).start()
         z_b(3, way).start()
     relay_b(0)
     pass_b(2, -2)
-    relay_a(1)
+    relay_a(3, 1, 2)
     whole_b(0)
     compute(0, 0)
     compute(0, 1)
     relay_b(1, -1)
-    compute(0, 2)
-    compute(0, 3)
     for way in (1, -1):
         z_b(4, way).wait_recv()
         z_b(3, way).wait_recv()
     pass_b(4, 3, -3)
-    relay_a(2)
+    compute(0, 2)
+    compute(0, 3)
     relay_b(2, -2)
     spread(0)
+    whole_a(1)
     whole_b(1, -1)
     compute(1, 0)
     compute(1, 1)
     relay_b(4, 3, -3)
-    relay_a(3)
     compute(1, 2)
     compute(1, 3)
     spread(1)
@@ -284,22 +317,17 @@
     spread(2)
     middle(1)
     finish(0)
-    whole_b(3, -3)
+    whole_a(3)
+    whole_a(4)
+    whole_b(4, 3, -3)
     for n in range(4):
         compute(3, n)
     spread(3)
     middle(2)
     finish(1)
-    relay_a(4)
-    whole_b(4)
-    for n in range(4):
-        compute(4, n)
-    spread(4)
     middle(3)
     finish(2)
-    middle(4)
     finish(3)
-    finish(4)
 
     for index in range(NB):
         for side in (1, -1):
@@ -310,7 +338,6 @@
     natural = jnp.zeros((ROWS, 1), jnp.int32)
     for r in range(ROWS):
         natural = jnp.where(rows_iota == r, place[r], natural)
-    low = lax.broadcasted_iota(jnp.int32, (ROWS, 128), 1) < 64
     for m in range(32):
         blocks = []
         for j in (2 * m, 2 * m + 1):
@@ -327,13 +354,11 @@
         one.wait_send()
 
 
-MESSAGES = 4 + 8 + 28 + 16 + 16 + 3 + 5 + 15 + 63
+MESSAGES = 4 + 8 + 28 + 16 + 16 + 3 + 4 + 12 + 63
 
 
 def shards(amplitudes, partner, integrals, pattern, owner):
     plain = amplitudes.reshape(ROWS, TT)
-    turned = jnp.swapaxes(plain.reshape(ROWS, 64, 64), 1, 2).reshape(ROWS, TT)
-    plain = jnp.where(lax.axis_index("pair") < NB * NY, plain, turned)
     vmem = pl.BlockSpec(memory_space=pltpu.VMEM)
     smem = pl.BlockSpec(memory_space=pltpu.SMEM)
     result = pl.pallas_call(

time: 72.2 us -> 68.8 us (0.953)
  other arithmetic: 1.48 us -> 0 us
  local copies, waits for them, and re-layouts: 3.03 us -> 1.7 us
    select_n x1 -> x0, other arithmetic: 1.48 us -> none  [shards(): plain = jnp.where(lax.axis_index('pair') < NB * NY, plain, turned)]
    another operation x2 -> x0, local copies, waits for them, and re-layouts: 1.15 us -> none  [shards(): turned = jnp.swapaxes(plain.reshape(ROWS, 64, 64), 1, 2).reshape(ROWS, TT)]
where the time goes in v3:
time: 68.8 us; the launch traced here: 68.6 us
  Pallas kernels  66.9 us (97%)
  local copies, waits for them, and re-layouts  1.7 us (2%)
    pallas_call x1, Pallas kernels, shards(): pl.pallas_call(kernel, out_shape=jax.ShapeDtypeStruct((2, ROWS, TT), jnp....  66.9 us
    transpose x1, local copies, waits for them, and re-layouts, shards(): return jnp.swapaxes(result, 0, 1)  1.7 us

profile of v3, /device:TPU:1, one launch (start us, length us, event | category | flops | bytes accessed | tf_op | source)
XLA Modules:
  0.0 68.6 jit_solution(9443298726009859995)
XLA Ops:
  0.0 66.9 %shard_map.55 = bf16[2,8,4096]{2,1,0:T(8,128)(2,1)} custom-call(bf16[8,4096]{1,0:T(8,128)(2,1)} %bitcast.5, bf16[512,4096]{1,0:T(8,128)(2,1)} %bitcast.3, s32[8]{0:T(128)} %partner.1, s32[8]{0:T(128)} %pattern.1, s32[16]{0:T(128)} %owner.1), custom_call_target="tpu_custom_call" | custom-call | tf_op jit(solution)/shard_map/pallas_call | solution.py:364
  67.0 1.7 %copy.6 = bf16[8,2,4096]{2,1,0:T(2,128)(2,1)} copy(bf16[8,2,4096]{2,0,1:T(8,128)(2,1)} %bitcast.4) | data formatting | bytes 262144 | tf_op jit(solution)/shard_map/transpose | solution.py:391

commit v4 on v3

--- a/solution.py
+++ b/solution.py
@@ -317,13 +317,13 @@
     spread(2)
     middle(1)
     finish(0)
+    middle(2)
     whole_a(3)
     whole_a(4)
     whole_b(4, 3, -3)
     for n in range(4):
         compute(3, n)
     spread(3)
-    middle(2)
     finish(1)
     middle(3)
     finish(2)

time: 68.8 us -> 68.1 us (0.990)
  Pallas kernels: 66.9 us -> 66.2 us
    pallas_call x1, Pallas kernels: 66.9 us -> 66.2 us  [shards(): pl.pallas_call(kernel, out_shape=jax.ShapeDtypeStruct((2, ROWS, TT), jnp....]
where the time goes in v4:
time: 68.1 us; the launch traced here: 67.9 us
  Pallas kernels  66.2 us (97%)
  local copies, waits for them, and re-layouts  1.7 us (2%)
    pallas_call x1, Pallas kernels, shards(): pl.pallas_call(kernel, out_shape=jax.ShapeDtypeStruct((2, ROWS, TT), jnp....  66.2 us
    transpose x1, local copies, waits for them, and re-layouts, shards(): return jnp.swapaxes(result, 0, 1)  1.7 us

profile of v4, /device:TPU:1, one launch (start us, length us, event | category | flops | bytes accessed | tf_op | source)
XLA Modules:
  0.0 67.9 jit_solution(10496849119807158534)
XLA Ops:
  0.0 66.2 %shard_map.55 = bf16[2,8,4096]{2,1,0:T(8,128)(2,1)} custom-call(bf16[8,4096]{1,0:T(8,128)(2,1)} %bitcast.5, bf16[512,4096]{1,0:T(8,128)(2,1)} %bitcast.3, s32[8]{0:T(128)} %partner.1, s32[8]{0:T(128)} %pattern.1, s32[16]{0:T(128)} %owner.1), custom_call_target="tpu_custom_call" | custom-call | tf_op jit(solution)/shard_map/pallas_call | solution.py:364
  66.2 1.7 %copy.6 = bf16[8,2,4096]{2,1,0:T(2,128)(2,1)} copy(bf16[8,2,4096]{2,0,1:T(8,128)(2,1)} %bitcast.4) | data formatting | bytes 262144 | tf_op jit(solution)/shard_map/transpose | solution.py:391

commit v5 on v4

--- a/solution.py
+++ b/solution.py
@@ -285,8 +285,8 @@
     relay_a(0)
     for way in (1, -1):
         z_b(2, way).wait_recv()
+        z_b(3, way).start()
         z_b(4, way).start()
-        z_b(3, way).start()
     relay_b(0)
     pass_b(2, -2)
     relay_a(3, 1, 2)
@@ -295,9 +295,11 @@
     compute(0, 1)
     relay_b(1, -1)
     for way in (1, -1):
+        z_b(3, way).wait_recv()
+    pass_b(3, -3)
+    for way in (1, -1):
         z_b(4, way).wait_recv()
-        z_b(3, way).wait_recv()
-    pass_b(4, 3, -3)
+    pass_b(4)
     compute(0, 2)
     compute(0, 3)
     relay_b(2, -2)
@@ -306,7 +308,7 @@
     whole_b(1, -1)
     compute(1, 0)
     compute(1, 1)
-    relay_b(4, 3, -3)
+    relay_b(3, -3, 4)
     compute(1, 2)
     compute(1, 3)
     spread(1)

time: 68.1 us -> 68.4 us (level)
  no operation moved by 1% of the time
where the time goes in v5:
time: 68.4 us; the launch traced here: 68.2 us
  Pallas kernels  66.5 us (97%)
  local copies, waits for them, and re-layouts  1.7 us (2%)
    pallas_call x1, Pallas kernels, shards(): pl.pallas_call(kernel, out_shape=jax.ShapeDtypeStruct((2, ROWS, TT), jnp....  66.5 us
    transpose x1, local copies, waits for them, and re-layouts, shards(): return jnp.swapaxes(result, 0, 1)  1.7 us

profile of v5, /device:TPU:1, one launch (start us, length us, event | category | flops | bytes accessed | tf_op | source)
XLA Modules:
  0.0 68.2 jit_solution(3721850992045732709)
XLA Ops:
  0.0 66.5 %shard_map.55 = bf16[2,8,4096]{2,1,0:T(8,128)(2,1)} custom-call(bf16[8,4096]{1,0:T(8,128)(2,1)} %bitcast.5, bf16[512,4096]{1,0:T(8,128)(2,1)} %bitcast.3, s32[8]{0:T(128)} %partner.1, s32[8]{0:T(128)} %pattern.1, s32[16]{0:T(128)} %owner.1), custom_call_target="tpu_custom_call" | custom-call | tf_op jit(solution)/shard_map/pallas_call | solution.py:366
  66.5 1.7 %copy.6 = bf16[8,2,4096]{2,1,0:T(2,128)(2,1)} copy(bf16[8,2,4096]{2,0,1:T(8,128)(2,1)} %bitcast.4) | data formatting | bytes 262144 | tf_op jit(solution)/shard_map/transpose | solution.py:393
